TPU v7x, 32 devices: a whole 2x2x4 slice. The times are simulated.
32 devices in a mesh: fsdp: 8 (over y, x, core), tp: 4 (over z).
Axes of the slice: x: 2, y: 2, z: 4, core: 2. Of those that a mesh axis runs over, the one named last changes fastest.
Arguments:
- pool: bfloat16 [1024, 16384], P(None, 'fsdp'), may hold values from -6 to 6
- ids: int32 [2, 384], replicated, may hold values from 0 to 1023, as said below
- gate_q: bfloat16 [26624, 16384], P(('fsdp', 'tp')), may hold values from -240 to 240, as said below
- up_q: bfloat16 [26624, 16384], P(('fsdp', 'tp')), may hold values from -240 to 240, as said below
- gate_scale: float32 [208, 128], replicated, may hold values from 3e-05 to 0.0003
- up_scale: float32 [208, 128], replicated, may hold values from 3e-05 to 0.0003
- down_weight: bfloat16 [26624, 16384], P('tp', 'fsdp'), may hold values from -0.0390625 to 0.0390625
Outputs:
- mixed: bfloat16 [2, 384, 16384], P(None, 'tp', 'fsdp')
Inputs may be any that keep to these rules, and one draw needn't show every extreme that they name: All 768 ids are different: no request is decoded twice. `gate_q`: every entry is a value of the 8-bit float form e4m3: a sign times (1 + k / 8) times 2 to the power e, with whole k of 0 to 7 and whole e of 0 to 7. `up_q`: every entry is a value of the 8-bit float form e4m3: a sign times (1 + k / 8) times 2 to the power e, with whole k of 0 to 7 and whole e of 0 to 7.
All inputs are finite; a program needn't handle non-finite values.
Results may differ from a plain program's by a relative error of at most 0.0065.
Values may be sent and summed in bfloat16 or wider, within the bound.
No kernel may reach another device: no remote copies, remote signals or barrier semaphores. Data moves between devices by JAX's collectives and lax.ppermute only.
A program may use at most 448 MiB of HBM per device.

v0:
```python
import jax
import jax.numpy as jnp
from jax import lax
from jax.sharding import PartitionSpec as P

BLOCK = 128


def broadcast(block, axis, owner):
    block = jnp.where(lax.axis_index(axis) == owner, block, jnp.zeros_like(block))
    return lax.psum(block, axis)


def project(hidden, down_weight):
    summed = lax.psum_scatter(
        jnp.dot(hidden, down_weight, preferred_element_type=jnp.float32),
        "tp",
        scatter_dimension=0,
        tiled=True,
    )
    return summed.astype(jnp.bfloat16)


def on_device(pool, ids, gate_q, up_q, gate_scale, up_scale, down_weight):
    n_fsdp = lax.axis_size("fsdp")
    n_tp = lax.axis_size("tp")
    fsdp_index = lax.axis_index("fsdp")
    tp_index = lax.axis_index("tp")
    scales = jnp.stack([gate_scale, up_scale])
    steps = ids.shape[0]
    results = []
    quant = jnp.stack([gate_q, up_q])
    rows_here = quant.shape[1]
    width = quant.shape[2]
    owner = fsdp_index * n_tp + tp_index
    row_blocks = (owner * rows_here + jnp.arange(rows_here, dtype=jnp.int32)) // BLOCK
    row_scales = jnp.take(scales, row_blocks, axis=1)
    weights = (
        (
            quant.astype(jnp.float32).reshape(2, rows_here, width // BLOCK, BLOCK)
            * row_scales[:, :, :, None]
        )
        .astype(jnp.bfloat16)
        .reshape(2, rows_here, width)
    )
    group = n_fsdp // n_tp
    for step in range(steps):
        tokens = jnp.take(pool, ids[step], axis=0)
        columns = weights
        both = jnp.einsum(
            "rd,gfd->rgf",
            lax.all_gather(tokens, "fsdp", axis=1, tiled=True),
            columns,
            preferred_element_type=jnp.float32,
        )
        hidden_own = (jax.nn.silu(both[:, 0]) * both[:, 1]).astype(jnp.bfloat16)
        grouped = lax.all_gather(hidden_own, "tp", axis=1, tiled=True)
        columns = []
        for member in range(group):
            columns.append(broadcast(grouped, "fsdp", group * tp_index + member))
        hidden = jnp.concatenate(columns, axis=1)
        results.append(project(hidden, down_weight))
    return jnp.stack(results)


def solution(mesh):
    in_specs = (
        P(None, "fsdp"),
        P(),
        P(("fsdp", "tp"), None),
        P(("fsdp", "tp"), None),
        P(),
        P(),
        P("tp", "fsdp"),
    )
    out_specs = P(None, "tp", "fsdp")
    return jax.shard_map(
        on_device, mesh=mesh, in_specs=in_specs, out_specs=out_specs, check_vma=False
    )
```

profile of v0, /device:TPU:0, one launch (start us, length us, event | category | flops | bytes accessed | tf_op | source)
XLA Modules:
  0.0 666.3 jit_solution(9128246473485798060)
XLA Ops:
  7.4 7.1 %gather_fusion.1 = bf16[384,2048]{1,0:T(8,128)(2,1)S(1)} fusion(bf16[1024,2048]{1,0:T(8,128)(2,1)} %param.9, s32[1024]{0:T(1024)S(1)} %pad_clamp_fusion.2), kind=kCustom, calls=%fused_computation.clone | custom fusion | bytes 3147264 | tf_op jit(solution)/shard_map/jit(_take)/gather | solution.py:48
  14.5 1.4 broadcast_select_fusion.5
  16.0 7.1 %gather_fusion.2 = bf16[384,2048]{1,0:T(8,128)(2,1)S(1)} fusion(bf16[1024,2048]{1,0:T(8,128)(2,1)} %param.9, s32[1024]{0:T(1024)S(1)} %pad_clamp_fusion), kind=kCustom, calls=%fused_computation.1.clone | custom fusion | bytes 3147264 | tf_op jit(solution)/shard_map/jit(_take)/gather | solution.py:48
  23.1 1.4 broadcast_select_fusion.4
  25.1 3.5 gather_fusion
  28.6 3.1 select_bitcast_fusion
  31.7 37.6 %mul.39 = f32[2,832,128,128]{3,2,1,0:T(8,128)} broadcast(f32[2,832,128]{2,1,0:T(8,128)S(1)} %copy.8), dimensions={0,1,2} | broadcast | bytes 109903872 | tf_op jit(solution)/shard_map/mul | solution.py:40
  69.3 116.0 %mul.40 = f32[2,832,16384]{2,1,0:T(8,128)} reshape(f32[2,832,128,128]{3,2,1,0:T(8,128)} %mul.39) | data formatting | bytes 218103808 | tf_op jit(solution)/shard_map/mul | solution.py:40
  185.2 60.5 %fusion.2 = f32[384,2,832]{0,2,1:T(8,128)S(1)} fusion(bf16[384,16384]{1,0:T(8,128)(2,1)} %all-gather.5.cloned.1.call-done, f32[2,832,16384]{2,1,0:T(8,128)} %mul.40, bf16[1,832,16384]{2,1,0:T(8,128)(2,1)} %bitcast.42, bf16[1,832,16384]{2,1,0:T(8,128)(2,1)} %bitcast.44), kind=kOutput, calls=%fused_computation.6 | convolution fusion | flops 21101543424 | bytes 178716672 | tf_op jit(solution)/shard_map/rd,gfd->rgf/dot_general | solution.py:50
  245.7 1.2 fusion.15
  247.1 61.2 %fusion = f32[384,2,832]{0,2,1:T(8,128)S(1)} fusion(bf16[384,16384]{1,0:T(8,128)(2,1)} %all-gather.9.cloned.1.call-done, f32[2,832,16384]{2,1,0:T(8,128)} %mul.40, bf16[1,832,16384]{2,1,0:T(8,128)(2,1)} %bitcast.43, bf16[1,832,16384]{2,1,0:T(8,128)(2,1)} %bitcast.45), kind=kOutput, calls=%fused_computation.4 | convolution fusion | flops 21101543424 | bytes 178716672 | tf_op jit(solution)/shard_map/rd,gfd->rgf/dot_general | solution.py:50
  308.2 1.2 fusion.13
  309.8 4.5 broadcast_select_fusion.3
  314.3 51.8 %all-gather.11.cloned.1.call-done = bf16[384,3328]{0,1:T(8,128)(2,1)} async-done(((bf16[384,832]{0,1:T(8,128)(2,1)}), bf16[384,3328]{0,1:T(8,128)(2,1)}) %all-gather.11.cloned.1.call-update) | async-done | bytes 2555920 | tf_op jit(solution)/shard_map/all_gather | solution.py:57
  366.0 4.4 broadcast_select_fusion.2
  370.5 145.1 %all-reduce.3.cloned.1.call-done = (bf16[384,3328]{0,1:T(8,128)(2,1)}, bf16[384,3328]{0,1:T(8,128)(2,1)}, bf16[384,3328]{0,1:T(8,128)(2,1)}, bf16[384,3328]{0,1:T(8,128)(2,1)}) async-done(((bf16[384,3328]{0,1:T(8,128)(2,1)}, bf16[384,3328]{0,1:T(8,128)(2,1)}, bf16[384,3328]{0,1:T(8,128)(2,1)}, bf16[384,3328]{0,1:T(8,128)(2,1)}), (bf16[384,3328]{0,1:T(8,128)(2,1)}, bf16[384,3328]{0,1:T(8,128)(2,1)}, ...) | async-done | bytes 10223632 | tf_op jit(solution)/shard_map/psum | solution.py:11
  515.6 18.4 %fusion.4 = f32[384,2048]{1,0:T(8,128)} fusion(bf16[6656,2048]{1,0:T(8,128)(2,1)} %param.15, bf16[384,3328]{0,1:T(8,128)(2,1)} %get-tuple-element.10, bf16[384,3328]{0,1:T(8,128)(2,1)} %get-tuple-element.11), kind=kOutput, calls=%fused_computation.8 | convolution fusion | flops 10479206400 | bytes 35520512 | tf_op jit(solution)/shard_map/dot_general | solution.py:16
  534.1 1.6 copy-done.2
  535.7 18.3 %fusion.8 = f32[384,2048]{1,0:T(8,128)} fusion(bf16[6656,2048]{1,0:T(8,128)(2,1)} %param.15, bf16[384,3328]{0,1:T(8,128)(2,1)S(1)} %copy-done.2, bf16[384,3328]{0,1:T(8,128)(2,1)} %get-tuple-element.9), kind=kOutput, calls=%fused_computation.12 | convolution fusion | flops 10479206400 | bytes 35520512 | tf_op jit(solution)/shard_map/dot_general | solution.py:16
  554.0 40.6 %reduce-scatter.3.cloned.1.call-done = f32[96,2048]{1,0:T(8,128)} async-done(((f32[384,2048]{1,0:T(8,128)}), f32[96,2048]{1,0:T(8,128)}) %reduce-scatter.3.cloned.1.call-update) | async-done | bytes 786448 | tf_op jit(solution)/shard_map/reduce_scatter | solution.py:15
  594.7 1.2 convert_bitcast_fusion.1
  595.9 61.5 %reduce-scatter.5.cloned.1.call-done = f32[96,2048]{1,0:T(8,128)} async-done(((f32[384,2048]{1,0:T(8,128)}), f32[96,2048]{1,0:T(8,128)}) %reduce-scatter.5.cloned.1.call-update) | async-done | bytes 786448 | tf_op jit(solution)/shard_map/reduce_scatter | solution.py:15
  657.3 1.2 convert_bitcast_fusion
  658.5 0.9 pad_maximum_fusion
  (34 shorter events, 2.0 us)
Async XLA Ops:
  6.5 178.7 %all-gather.5.cloned.1.call-start = ((), (), s32[]{:S(2)}) async-start(), calls=%async_computation.2 | async-start | bytes 14155776 | tf_op jit(solution)/shard_map/all_gather | solution.py:52
  15.9 231.2 %all-gather.9.cloned.1.call-start = ((), (), s32[]{:S(2)}) async-start(), calls=%async_computation.5 | async-start | bytes 14155776 | tf_op jit(solution)/shard_map/all_gather | solution.py:52
  23.1 1.8 copy-start
  23.1 1.7 copy-start.1
  24.5 285.2 %all-gather.7.cloned.1.call-start = ((), (), s32[]{:S(2)}) async-start(), calls=%async_computation.3 | async-start | bytes 3194880 | tf_op jit(solution)/shard_map/all_gather | solution.py:57
  247.0 119.0 %all-gather.11.cloned.1.call-start = ((), (), s32[]{:S(2)}) async-start(), calls=%async_computation.6 | async-start | bytes 3194880 | tf_op jit(solution)/shard_map/all_gather | solution.py:57
  309.5 206.2 %all-reduce.3.cloned.1.call-start = ((), (), s32[]{:S(2)}) async-start(), calls=%async_computation.8 | async-start | bytes 20447232 | tf_op jit(solution)/shard_map/psum | solution.py:11
  370.4 224.2 %reduce-scatter.3.cloned.1.call-start = ((), (), s32[]{:S(2)}) async-start(), calls=%async_computation.4 | async-start | bytes 3932160 | tf_op jit(solution)/shard_map/reduce_scatter | solution.py:15
  534.0 1.7 copy-start.2
  534.0 123.3 %reduce-scatter.5.cloned.1.call-start = ((), (), s32[]{:S(2)}) async-start(), calls=%async_computation.7 | async-start | bytes 3932160 | tf_op jit(solution)/shard_map/reduce_scatter | solution.py:15
Sparse Core Ops, SparseCore 0:
  16.0 74.7 all-gather.4
  92.7 71.9 all-gather.8
  247.1 56.3 all-gather.6
  309.6 56.3 all-gather.10
  370.6 144.9 all-reduce.2
  534.2 60.4 reduce-scatter.2
  597.0 60.3 reduce-scatter.4
where the time goes:
time: 670 us; the launch traced here: 666 us
  waiting for transfers between devices  299 us (45%)
  local copies, waits for them, and re-layouts  174 us (26%)
  matrix products  158 us (24%)
  other arithmetic  20.7 us (3%)
  between operations  13.7 us (2%)
    mul x2, local copies, waits for them, and re-layouts, on_device(): quant.astype(jnp.float32).reshape(2, rows_here, width // BLOCK, BLOCK)  154 us
    psum x1, waiting for transfers between devices, broadcast(): return lax.psum(block, axis)  145 us
    dot_general x2, matrix products, on_device(): jnp.einsum('rd,gfd->rgf', lax.all_gather(tokens, 'fsdp', axis=1, tiled=Tr...  122 us
    reduce_scatter x2, waiting for transfers between devices, project(): lax.psum_scatter(jnp.dot(hidden, down_weight, preferred_element_type=jnp....  102 us
    all_gather x2, waiting for transfers between devices, on_device(): grouped = lax.all_gather(hidden_own, 'tp', axis=1, tiled=True)  51.8 us
    dot_general x2, matrix products, project(): jnp.dot(hidden, down_weight, preferred_element_type=jnp.float32)  36.7 us
    gather x2, local copies, waits for them, and re-layouts, on_device(): tokens = jnp.take(pool, ids[step], axis=0)  14.2 us
  transfers between devices with their start and end apart: 7, of which 4 were waited for; matrix products, arithmetic and copies ran while one was open for 48% of the time, Pallas kernels for 0%

commit v1 on v0

--- a/solution.py
+++ b/solution.py
@@ -8,7 +8,7 @@
 
 def broadcast(block, axis, owner):
     block = jnp.where(lax.axis_index(axis) == owner, block, jnp.zeros_like(block))
-    return lax.psum(block, axis)
+    return jnp.sum(lax.all_gather(block, axis), axis=0)
 
 
 def project(hidden, down_weight):

time: 670 us -> 960 us (1.43)
  waiting for transfers between devices: 299 us -> 438 us
  local copies, waits for them, and re-layouts: 174 us -> 252 us
  other arithmetic: 20.7 us -> 78 us
  matrix products: 158 us -> 168 us
    all_gather x0 -> x4, waiting for transfers between devices: none -> 325 us  [broadcast(): return jnp.sum(lax.all_gather(block, axis), axis=0)]
    psum x1 -> x0, waiting for transfers between devices: 145 us -> none  [broadcast(): return lax.psum(block, axis)]
    unnamed x6 -> x12, local copies, waits for them, and re-layouts: 1.66 us -> 80.3 us
    reduce_sum x0 -> x2, other arithmetic: none -> 57.4 us  [broadcast(): return jnp.sum(lax.all_gather(block, axis), axis=0)]
    reduce_scatter x2, waiting for transfers between devices: 102 us -> 59.5 us  [project(): lax.psum_scatter(jnp.dot(hidden, down_weight, preferred_element_type=jnp....]
    dot_general x2, matrix products: 36.7 us -> 46.6 us  [project(): jnp.dot(hidden, down_weight, preferred_element_type=jnp.float32)]
  transfers between devices with their start and end apart: 7 -> 10, of which waited for: 4 -> 6; matrix products, arithmetic and copies ran while one was open for 48% -> 51% of each run, Pallas kernels for 0% -> 0%
where the time goes in v1:
time: 960 us; the launch traced here: 952 us
  waiting for transfers between devices  438 us (46%)
  local copies, waits for them, and re-layouts  252 us (26%)
  matrix products  168 us (18%)
  other arithmetic  78 us (8%)
  between operations  14 us (1%)
    all_gather x4, waiting for transfers between devices, broadcast(): return jnp.sum(lax.all_gather(block, axis), axis=0)  325 us
    mul x2, local copies, waits for them, and re-layouts, on_device(): quant.astype(jnp.float32).reshape(2, rows_here, width // BLOCK, BLOCK)  153 us
    dot_general x2, matrix products, on_device(): jnp.einsum('rd,gfd->rgf', lax.all_gather(tokens, 'fsdp', axis=1, tiled=Tr...  122 us
    unnamed x12, local copies, waits for them, and re-layouts  80.3 us
    reduce_scatter x2, waiting for transfers between devices, project(): lax.psum_scatter(jnp.dot(hidden, down_weight, preferred_element_type=jnp....  59.5 us
    reduce_sum x2, other arithmetic, broadcast(): return jnp.sum(lax.all_gather(block, axis), axis=0)  57.4 us
    all_gather x2, waiting for transfers between devices, on_device(): grouped = lax.all_gather(hidden_own, 'tp', axis=1, tiled=True)  51.4 us
    dot_general x2, matrix products, project(): jnp.dot(hidden, down_weight, preferred_element_type=jnp.float32)  46.6 us
  transfers between devices with their start and end apart: 10, of which 6 were waited for; matrix products, arithmetic and copies ran while one was open for 51% of the time, Pallas kernels for 0%

profile of v1, /device:TPU:0, one launch (start us, length us, event | category | flops | bytes accessed | tf_op | source)
XLA Modules:
  0.0 951.5 jit_solution(7174265848508875846)
XLA Ops:
  7.4 7.1 gather_fusion.1
  15.9 7.1 gather_fusion.2
  25.3 3.5 gather_fusion
  28.9 3.1 select_bitcast_fusion
  32.0 37.6 %mul.39 = f32[2,832,128,128]{3,2,1,0:T(8,128)} broadcast(f32[2,832,128]{2,1,0:T(8,128)S(1)} %copy.9), dimensions={0,1,2} | broadcast | bytes 109903872 | tf_op jit(solution)/shard_map/mul | solution.py:40
  69.5 115.9 %mul.40 = f32[2,832,16384]{2,1,0:T(8,128)} reshape(f32[2,832,128,128]{3,2,1,0:T(8,128)} %mul.39) | data formatting | bytes 218103808 | tf_op jit(solution)/shard_map/mul | solution.py:40
  185.4 60.5 %fusion.2 = f32[384,2,832]{0,2,1:T(8,128)S(1)} fusion(bf16[384,16384]{1,0:T(8,128)(2,1)} %all-gather.13.cloned.1.call-done, f32[2,832,16384]{2,1,0:T(8,128)} %mul.40, bf16[1,832,16384]{2,1,0:T(8,128)(2,1)} %bitcast.66, bf16[1,832,16384]{2,1,0:T(8,128)(2,1)} %bitcast.68), kind=kOutput, calls=%fused_computation.10 | convolution fusion | flops 21101543424 | bytes 178716672 | tf_op jit(solution)/shard_map/rd,gfd->rgf/dot_general | solution.py:50
  247.2 61.2 %fusion = f32[384,2,832]{0,2,1:T(8,128)S(1)} fusion(bf16[384,16384]{1,0:T(8,128)(2,1)} %all-gather.17.cloned.1.call-done, f32[2,832,16384]{2,1,0:T(8,128)} %mul.40, bf16[1,832,16384]{2,1,0:T(8,128)(2,1)} %bitcast.67, bf16[1,832,16384]{2,1,0:T(8,128)(2,1)} %bitcast.69), kind=kOutput, calls=%fused_computation.8 | convolution fusion | flops 21101543424 | bytes 178716672 | tf_op jit(solution)/shard_map/rd,gfd->rgf/dot_general | solution.py:50
  309.8 4.5 broadcast_select_fusion.3
  314.9 51.4 %all-gather.19.cloned.1.call-done = bf16[384,3328]{0,1:T(8,128)(2,1)} async-done(((bf16[384,832]{0,1:T(8,128)(2,1)}), bf16[384,3328]{0,1:T(8,128)(2,1)}) %all-gather.19.cloned.1.call-update) | async-done | bytes 2555920 | tf_op jit(solution)/shard_map/all_gather | solution.py:57
  366.3 4.4 broadcast_select_fusion.2
  371.5 104.6 %all-gather.21.cloned.1.call-done = bf16[3072,3328]{0,1:T(8,128)(2,1)} async-done(((bf16[384,3328]{0,1:T(8,128)(2,1)}), bf16[3072,3328]{0,1:T(8,128)(2,1)}) %all-gather.21.cloned.1.call-update) | async-done | bytes 20447248 | tf_op jit(solution)/shard_map/all_gather | solution.py:11
  476.1 19.0 %copy.10 = bf16[416,8,8,384]{3,2,1,0:T(8,128)(2,1)} copy(bf16[416,8,8,384]{3,1,2,0:T(8,128)(2,1)} %bitcast.60) | data formatting | bytes 40894464
  495.2 92.0 %all-gather.23.cloned.1.call-done = bf16[3072,3328]{0,1:T(8,128)(2,1)} async-done(((bf16[384,3328]{0,1:T(8,128)(2,1)}), bf16[3072,3328]{0,1:T(8,128)(2,1)}) %all-gather.23.cloned.1.call-update) | async-done | bytes 20447248 | tf_op jit(solution)/shard_map/all_gather | solution.py:11
  587.2 20.9 %copy.11 = bf16[416,8,8,384]{3,2,1,0:T(8,128)(2,1)} copy(bf16[416,8,8,384]{3,1,2,0:T(8,128)(2,1)} %bitcast.62) | data formatting | bytes 40894464
  609.1 28.7 %bitcast_reduce_fusion.2 = (bf16[384,3328]{0,1:T(8,128)(2,1)S(1)}, bf16[384,3328]{0,1:T(8,128)(2,1)S(1)}) fusion(bf16[416,8,8,384]{3,2,1,0:T(8,128)(2,1)} %copy.11, bf16[416,8,8,384]{3,2,1,0:T(8,128)(2,1)S(1)} %copy-done), kind=kLoop, calls=%fused_computation.6 | loop fusion | flops 17891328 | bytes 46006272 | tf_op jit(solution)/shard_map/reduce_sum | solution.py:11
  637.8 23.5 %fusion.4 = f32[384,2048]{1,0:T(8,128)} fusion(bf16[6656,2048]{1,0:T(8,128)(2,1)} %param.15, bf16[384,3328]{0,1:T(8,128)(2,1)S(1)} %get-tuple-element.14, bf16[384,3328]{0,1:T(8,128)(2,1)S(1)} %get-tuple-element.15), kind=kOutput, calls=%fused_computation.12 | convolution fusion | flops 10479206400 | bytes 35520512 | tf_op jit(solution)/shard_map/dot_general | solution.py:16
  661.6 36.8 %all-gather.25.cloned.1.call-done = bf16[3072,3328]{0,1:T(8,128)(2,1)} async-done(((bf16[384,3328]{0,1:T(8,128)(2,1)}), bf16[3072,3328]{0,1:T(8,128)(2,1)}) %all-gather.25.cloned.1.call-update) | async-done | bytes 20447248 | tf_op jit(solution)/shard_map/all_gather | solution.py:11
  698.3 19.1 %copy.12 = bf16[416,8,8,384]{3,2,1,0:T(8,128)(2,1)} copy(bf16[416,8,8,384]{3,1,2,0:T(8,128)(2,1)} %bitcast.61) | data formatting | bytes 40894464
  717.4 92.1 %all-gather.27.cloned.1.call-done = bf16[3072,3328]{0,1:T(8,128)(2,1)} async-done(((bf16[384,3328]{0,1:T(8,128)(2,1)}), bf16[3072,3328]{0,1:T(8,128)(2,1)}) %all-gather.27.cloned.1.call-update) | async-done | bytes 20447248 | tf_op jit(solution)/shard_map/all_gather | solution.py:11
  809.5 20.3 %copy.13 = bf16[416,8,8,384]{3,2,1,0:T(8,128)(2,1)} copy(bf16[416,8,8,384]{3,1,2,0:T(8,128)(2,1)} %bitcast.63) | data formatting | bytes 40894464
  829.8 28.7 %bitcast_reduce_fusion = (bf16[384,3328]{0,1:T(8,128)(2,1)S(1)}, bf16[384,3328]{0,1:T(8,128)(2,1)S(1)}) fusion(bf16[416,8,8,384]{3,2,1,0:T(8,128)(2,1)} %copy.13, bf16[416,8,8,384]{3,2,1,0:T(8,128)(2,1)S(1)} %copy-done.1), kind=kLoop, calls=%fused_computation.4 | loop fusion | flops 17891328 | bytes 46006272 | tf_op jit(solution)/shard_map/reduce_sum | solution.py:11
  858.5 23.1 %fusion.8 = f32[384,2048]{1,0:T(8,128)} fusion(bf16[6656,2048]{1,0:T(8,128)(2,1)} %param.15, bf16[384,3328]{0,1:T(8,128)(2,1)S(1)} %get-tuple-element.12, bf16[384,3328]{0,1:T(8,128)(2,1)S(1)} %get-tuple-element.13), kind=kOutput, calls=%fused_computation.16 | convolution fusion | flops 10479206400 | bytes 35520512 | tf_op jit(solution)/shard_map/dot_general | solution.py:16
  882.8 59.5 %reduce-scatter.5.cloned.1.call-done = f32[96,2048]{1,0:T(8,128)} async-done(((f32[384,2048]{1,0:T(8,128)}), f32[96,2048]{1,0:T(8,128)}) %reduce-scatter.5.cloned.1.call-update) | async-done | bytes 786448 | tf_op jit(solution)/shard_map/reduce_scatter | solution.py:15
  (51 shorter events, 13.2 us)
Async XLA Ops:
  6.5 178.9 %all-gather.13.cloned.1.call-start = ((), (), s32[]{:S(2)}) async-start(), calls=%async_computation.2 | async-start | bytes 14155776 | tf_op jit(solution)/shard_map/all_gather | solution.py:52
  15.9 231.3 %all-gather.17.cloned.1.call-start = ((), (), s32[]{:S(2)}) async-start(), calls=%async_computation.5 | async-start | bytes 14155776 | tf_op jit(solution)/shard_map/all_gather | solution.py:52
  23.1 2.0 copy-start.2
  23.1 2.0 copy-start.3
  24.5 285.3 %all-gather.15.cloned.1.call-start = ((), (), s32[]{:S(2)}) async-start(), calls=%async_computation.3 | async-start | bytes 3194880 | tf_op jit(solution)/shard_map/all_gather | solution.py:57
  247.1 119.2 %all-gather.19.cloned.1.call-start = ((), (), s32[]{:S(2)}) async-start(), calls=%async_computation.6 | async-start | bytes 3194880 | tf_op jit(solution)/shard_map/all_gather | solution.py:57
  309.6 166.6 %all-gather.21.cloned.1.call-start = ((), (), s32[]{:S(2)}) async-start(), calls=%async_computation.8 | async-start | bytes 23003136 | tf_op jit(solution)/shard_map/all_gather | solution.py:11
  314.3 272.9 %all-gather.23.cloned.1.call-start = ((), (), s32[]{:S(2)}) async-start(), calls=%async_computation.9 | async-start | bytes 23003136 | tf_op jit(solution)/shard_map/all_gather | solution.py:11
  314.9 383.4 %all-gather.25.cloned.1.call-start = ((), (), s32[]{:S(2)}) async-start(), calls=%async_computation.10 | async-start | bytes 23003136 | tf_op jit(solution)/shard_map/all_gather | solution.py:11
  370.7 438.8 %all-gather.27.cloned.1.call-start = ((), (), s32[]{:S(2)}) async-start(), calls=%async_computation.11 | async-start | bytes 23003136 | tf_op jit(solution)/shard_map/all_gather | solution.py:11
  371.5 510.2 %reduce-scatter.3.cloned.1.call-start = ((), (), s32[]{:S(2)}) async-start(), calls=%async_computation.4 | async-start | bytes 3932160 | tf_op jit(solution)/shard_map/reduce_scatter | solution.py:15
  587.2 21.9 %copy-start = (bf16[416,8,8,384]{3,2,1,0:T(8,128)(2,1)S(1)}, bf16[416,8,8,384]{3,2,1,0:T(8,128)(2,1)}, u32[]{:S(2)}) copy-start(bf16[416,8,8,384]{3,2,1,0:T(8,128)(2,1)} %copy.10) | copy-start | bytes 61341700
  661.3 281.0 %reduce-scatter.5.cloned.1.call-start = ((), (), s32[]{:S(2)}) async-start(), calls=%async_computation.7 | async-start | bytes 3932160 | tf_op jit(solution)/shard_map/reduce_scatter | solution.py:15
  809.5 20.3 %copy-start.1 = (bf16[416,8,8,384]{3,2,1,0:T(8,128)(2,1)S(1)}, bf16[416,8,8,384]{3,2,1,0:T(8,128)(2,1)}, u32[]{:S(2)}) copy-start(bf16[416,8,8,384]{3,2,1,0:T(8,128)(2,1)} %copy.12) | copy-start | bytes 61341700
Sparse Core Ops, SparseCore 0:
  16.0 74.7 all-gather.12
  92.6 71.9 all-gather.16
  247.2 56.5 all-gather.14
  309.7 56.5 all-gather.18
  368.0 108.0 all-gather.20
  477.9 109.2 all-gather.22
  589.0 109.2 all-gather.24
  700.2 109.2 all-gather.26
  811.8 60.3 reduce-scatter.2
  881.7 60.5 reduce-scatter.4
